TPU v7x, 32 devices: a whole 2x2x4 slice. The times are simulated.
32 devices in a mesh: aux: 2 (over x), pair: 16 (over z, y, core).
Axes of the slice: x: 2, y: 2, z: 4, core: 2. Of those that a mesh axis runs over, the one named last changes fastest.
Arguments:
- three_index: bfloat16 [256, 256, 2048], P('pair', None, 'aux'), may hold values from -0.875 to 0.875
- fock_diag: float32 [256], replicated, may hold values from -1.2 to -0.3
- pair_occ: int32 [496, 2], P('pair'), may hold values from 0 to 255, as said below
- pno_count: int32 [496], P('pair'), may hold values from 32 to 128
- pno_energy: float32 [496, 128], P('pair'), may hold values from 0.3 to 3
- pno_coef: bfloat16 [496, 2, 256, 128], P('pair'), may hold values from -0.375 to 0.375
Outputs:
- pair_energy: float32 [496], P('pair')
- grad_ints: float32 [256, 256, 2048], P('pair', None, 'aux')
Inputs may be any that keep to these rules, and one draw needn't show every extreme that they name: `pair_occ`: orbital o belongs to the block o // 16. Among the 62 orbitals named by the pairs of one aligned block of 31 rows, at most 4 belong to any one orbital block, and one orbital block receives exactly 4 from every such row block; i may equal j.
All inputs are finite; a program needn't handle non-finite values.
Results may differ from a plain program's by a relative error of at most 0.0061.
Values may be sent and summed in bfloat16 or wider, within the bound.
No kernel may reach another device: no remote copies, remote signals or barrier semaphores. Data moves between devices by JAX's collectives and lax.ppermute only.
A program may use at most 128 MiB of HBM per device.

v0:
```python
import jax
import jax.numpy as jnp
from jax import lax
from jax.sharding import PartitionSpec as P


def local(three_index, fock_diag, pair_occ, pno_count, pno_energy, pno_coef):
    groups = lax.axis_size("pair")
    occ_dev = three_index.shape[0]
    width_dom = three_index.shape[1]
    width_aux = three_index.shape[2]
    pair_dev = pair_occ.shape[0]
    width_pno = pno_coef.shape[3]
    halves = 2 * pair_dev
    capacity = max(2, halves // groups + 1)
    slots = groups * capacity
    occ_flat = pair_occ.reshape(halves)
    owner_of = occ_flat // occ_dev
    local_index = occ_flat % occ_dev
    owner_hot = (owner_of[:, None] == jnp.arange(groups, dtype=jnp.int32)[None, :]).astype(
        jnp.int32
    )
    before = jnp.cumsum(owner_hot, axis=0) - owner_hot
    rank_in = jnp.sum(before * owner_hot, axis=1)
    slot_of = owner_of * capacity + rank_in
    request = jnp.zeros((slots,), jnp.int32).at[slot_of].set(local_index + 1)
    arrived = lax.all_to_all(
        request.reshape(groups, capacity), "pair", split_axis=0, concat_axis=0, tiled=True
    ).reshape(slots)
    is_live = arrived > 0
    row_index = jnp.maximum(arrived - 1, 0)
    selected = jnp.take(three_index, row_index, axis=0)
    selected = jnp.where(is_live[:, None, None], selected, jnp.zeros_like(selected))
    coef_half = pno_coef.reshape(halves, width_dom, width_pno)
    coef_send = jnp.zeros((slots, width_dom, width_pno), jnp.bfloat16).at[slot_of].set(coef_half)
    coef_recv = lax.all_to_all(
        coef_send.reshape(groups, capacity, width_dom, width_pno),
        "pair",
        split_axis=0,
        concat_axis=0,
        tiled=True,
    )
    coef_recv = coef_recv.reshape(slots, width_dom, width_pno)
    proj_here = jnp.einsum(
        "sdp,sdq->spq", coef_recv, selected, preferred_element_type=jnp.float32
    ).astype(jnp.bfloat16)
    proj_back = lax.all_to_all(
        proj_here.reshape(groups, capacity, width_pno, width_aux),
        "pair",
        split_axis=0,
        concat_axis=0,
        tiled=True,
    )
    projected = jnp.take(proj_back.reshape(slots, width_pno, width_aux), slot_of, axis=0)
    paired = projected.reshape(pair_dev, 2, width_pno, width_aux)
    rows_i = paired[:, 0]
    rows_j = paired[:, 1]
    partial_sum = jnp.einsum("kpq,krq->kpr", rows_i, rows_j, preferred_element_type=jnp.float32)
    coupling = lax.psum(partial_sum, "aux")
    fock_i = jnp.take(fock_diag, pair_occ[:, 0])
    fock_j = jnp.take(fock_diag, pair_occ[:, 1])
    denom = pno_energy[:, :, None] + pno_energy[:, None, :] - (fock_i + fock_j)[:, None, None]
    in_pno = jnp.arange(width_pno, dtype=jnp.int32)[None, :] < pno_count[:, None]
    both_in = in_pno[:, :, None] & in_pno[:, None, :]
    amplitude = jnp.where(both_in, -coupling / denom, jnp.float32(0.0))
    mixed = 2.0 * amplitude - jnp.swapaxes(amplitude, 1, 2)
    energy = jnp.sum(coupling * mixed, axis=(1, 2)) / (width_pno * width_pno)
    weights = mixed.astype(jnp.bfloat16)
    gamma_i = jnp.einsum(
        "kab,kbq->kaq", weights, rows_j, preferred_element_type=jnp.float32
    ).astype(jnp.bfloat16)
    gamma_j = jnp.einsum(
        "kba,kbq->kaq", weights, rows_i, preferred_element_type=jnp.float32
    ).astype(jnp.bfloat16)
    gamma = jnp.stack([gamma_i, gamma_j], axis=1).reshape(halves, width_pno, width_aux)
    gamma_send = jnp.zeros((slots, width_pno, width_aux), jnp.bfloat16).at[slot_of].set(gamma)
    gamma_recv = lax.all_to_all(
        gamma_send.reshape(groups, capacity, width_pno, width_aux),
        "pair",
        split_axis=0,
        concat_axis=0,
        tiled=True,
    )
    gamma_recv = gamma_recv.reshape(slots, width_pno, width_aux)
    terms = jnp.einsum(
        "sdp,spq->sdq", coef_recv, gamma_recv, preferred_element_type=jnp.float32
    ).astype(jnp.bfloat16)
    occ_hot = (row_index[None, :] == jnp.arange(occ_dev, dtype=jnp.int32)[:, None]) & is_live[
        None, :
    ]
    grad = jnp.dot(
        occ_hot.astype(jnp.bfloat16),
        terms.reshape(slots, width_dom * width_aux),
        preferred_element_type=jnp.float32,
    )
    return (energy, grad.reshape(occ_dev, width_dom, width_aux))


def solution(mesh):
    placed = (
        P("pair", None, "aux"),
        P(),
        P("pair", None),
        P("pair"),
        P("pair", None),
        P("pair", None, None, None),
    )
    return jax.shard_map(
        local,
        mesh=mesh,
        in_specs=placed,
        out_specs=(P("pair"), P("pair", None, "aux")),
        check_vma=False,
    )
```

profile of v0, /device:TPU:13, one launch (start us, length us, event | category | flops | bytes accessed | tf_op | source)
XLA Modules:
  0.0 1180.7 jit_solution(13151449799421802586)
XLA Ops:
  10.0 6.5 all-to-all-start.1
  19.6 11.7 scatter_fusion
  31.3 6.4 copy.56
  37.7 6.0 all-to-all-start
  44.0 15.7 %gather_fusion = bf16[64,256,1024]{2,1,0:T(8,128)(2,1)} fusion(bf16[16,256,1024]{2,1,0:T(8,128)(2,1)} %param.8, s32[1024]{0:T(1024)S(1)} %pad_clamp_fusion.3), kind=kCustom, calls=%fused_computation.2 | custom fusion | bytes 67109120 | tf_op jit(solution)/shard_map/jit(_take)/gather | solution.py:32
  59.7 76.5 %all-to-all-done = bf16[16,4,256,128]{2,3,1,0:T(8,128)(2,1)} async-done(((bf16[16,4,256,128]{2,3,1,0:T(8,128)(2,1)}), bf16[16,4,256,128]{2,3,1,0:T(8,128)(2,1)}, u32[]{:S(2)}, u32[]{:S(2)}) %all-to-all-start) | async-done | bytes 4194336 | tf_op jit(solution)/shard_map/all_to_all | solution.py:36
  136.2 18.3 %fusion.10 = bf16[64,128,1024]{2,1,0:T(8,128)(2,1)} fusion(bf16[64,256,128]{1,2,0:T(8,128)(2,1)} %bitcast.4, bf16[64,256,1024]{2,1,0:T(8,128)(2,1)} %gather_fusion, pred[64]{0:T(512)(128)(4,1)S(1)} %broadcast_compare_fusion, pred[64]{0:T(512)(128)(4,1)S(1)} %gt.15), kind=kOutput, calls=%fused_computation.20 | convolution fusion | flops 4336910336 | bytes 54526080 | tf_op jit(solution)/shard_map/sdp,sdq->spq/dot_general | solution.py:44
  154.5 5.2 all-to-all-start.2
  160.1 361.4 %all-to-all-done.2 = bf16[16,4,128,1024]{3,2,1,0:T(8,128)(2,1)} async-done(((bf16[16,4,128,1024]{3,2,1,0:T(8,128)(2,1)}), bf16[16,4,128,1024]{3,2,1,0:T(8,128)(2,1)}, u32[]{:S(2)}, u32[]{:S(2)}) %all-to-all-start.2) | async-done | bytes 16777248 | tf_op jit(solution)/shard_map/all_to_all | solution.py:47
  521.5 13.3 %gather_fusion.1 = bf16[62,128,1024]{2,1,0:T(8,128)(2,1)} fusion(bf16[64,128,1024]{2,1,0:T(8,128)(2,1)} %bitcast.7, s32[1024]{0:T(1024)S(1)} %pad_clamp_fusion.2), kind=kCustom, calls=%fused_computation.3 | custom fusion | bytes 32506104 | tf_op jit(solution)/shard_map/jit(_take)/gather | solution.py:54
  534.8 13.8 %copy_select_fusion = bf16[31,2,128,1024]{3,2,0,1:T(8,128)(2,1)} fusion(bf16[31,2,128,1024]{3,2,1,0:T(8,128)(2,1)} %bitcast.68, pred[31,2]{0,1:T(4,128)(4,1)S(1)} %compare_and_fusion), kind=kLoop, calls=%fused_computation.19 | loop fusion | flops 8126464 | bytes 32505918 | tf_op jit(solution)/shard_map/jit(_take)/select_n | solution.py:54
  548.7 9.2 fusion.14
  559.5 59.4 %all-reduce.2.cloned.1.call-done = f32[31,128,128]{2,1,0:T(8,128)} async-done(((f32[31,128,128]{2,1,0:T(8,128)}), f32[31,128,128]{2,1,0:T(8,128)}) %all-reduce.2.cloned.1.call-update) | async-done | bytes 2031632 | tf_op jit(solution)/shard_map/psum | solution.py:59
  630.5 5.6 convert_bitcast_fusion.1
  636.1 8.9 convert_bitcast_fusion
  645.0 6.2 pad_maximum_fusion
  651.2 6.4 copy.62
  657.6 6.1 broadcast_in_dim.68
  663.7 41.4 %scatter_fusion.1 = bf16[64,128,1024]{2,1,0:T(8,128)(2,1)} fusion(bf16[64,128,1024]{2,1,0:T(8,128)(2,1)} %broadcast_in_dim.68, s32[62]{0:T(128)S(1)} %fusion.25, bf16[62,128,1024]{2,1,0:T(8,128)(2,1)} %bitcast.67), kind=kCustom, calls=%fused_computation.6 | custom fusion | bytes 48759032 | tf_op jit(solution)/shard_map/scatter | solution.py:76
  705.1 6.5 all-to-all-start.3
  712.1 361.6 %all-to-all-done.3 = bf16[16,4,128,1024]{3,2,1,0:T(8,128)(2,1)} async-done(((bf16[16,4,128,1024]{3,2,1,0:T(8,128)(2,1)}), bf16[16,4,128,1024]{3,2,1,0:T(8,128)(2,1)}, u32[]{:S(2)}, u32[]{:S(2)}) %all-to-all-start.3) | async-done | bytes 16777248 | tf_op jit(solution)/shard_map/all_to_all | solution.py:77
  1073.7 21.3 %convolution_convert_fusion = bf16[64,256,1024]{2,1,0:T(8,128)(2,1)} fusion(bf16[64,256,128]{1,2,0:T(8,128)(2,1)} %bitcast.4, bf16[64,128,1024]{2,1,0:T(8,128)(2,1)} %bitcast.19), kind=kOutput, calls=%fused_computation.15 | convolution fusion | flops 4311744512 | bytes 54525952 | tf_op jit(solution)/shard_map/sdp,spq->sdq/dot_general | solution.py:85
  1095.0 60.6 %fusion = f32[16,256,1024]{2,0,1:T(8,128)} fusion(s32[64]{0:T(128)S(1)} %max.23, pred[64]{0:T(512)(128)(4,1)S(1)} %gt.15, bf16[8,8,256,1024]{3,2,1,0:T(8,128)(2,1)} %bitcast.65), kind=kOutput, calls=%fused_computation.7 | convolution fusion | flops 536872960 | bytes 50331968 | tf_op jit(solution)/shard_map/dot_general | solution.py:91
  1155.6 17.8 %copy.65 = f32[16,256,1024]{2,1,0:T(8,128)} copy(f32[16,256,1024]{2,0,1:T(8,128)} %fusion) | data formatting | bytes 33554432
  (45 shorter events, 20.2 us)
Async XLA Ops:
  7.2 550.8 %copy-start = (f32[256]{0:T(256)S(1)}, f32[256]{0:T(256)}, u32[]{:S(2)}) copy-start(f32[256]{0:T(256)} %param.9) | copy-start | bytes 3076
  10.0 27.7 %all-to-all-start.1 = ((s32[16,1,4]{2,1,0:T(1,128)}), s32[16,1,4]{2,1,0:T(1,128)S(1)}, u32[]{:S(2)}, u32[]{:S(2)}) async-start(s32[16,1,4]{2,1,0:T(1,128)} %bitcast.5), calls=%async_computation.1 | async-start | bytes 16384 | tf_op jit(solution)/shard_map/all_to_all | solution.py:27
  37.7 98.5 %all-to-all-start = ((bf16[16,4,256,128]{2,3,1,0:T(8,128)(2,1)}), bf16[16,4,256,128]{2,3,1,0:T(8,128)(2,1)}, u32[]{:S(2)}, u32[]{:S(2)}) async-start(bf16[16,4,256,128]{2,3,1,0:T(8,128)(2,1)} %copy.56), calls=%async_computation | async-start | bytes 8388608 | tf_op jit(solution)/shard_map/all_to_all | solution.py:36
  154.5 5.6 copy-start.3
  154.5 367.0 %all-to-all-start.2 = ((bf16[16,4,128,1024]{3,2,1,0:T(8,128)(2,1)}), bf16[16,4,128,1024]{3,2,1,0:T(8,128)(2,1)}, u32[]{:S(2)}, u32[]{:S(2)}) async-start(bf16[16,4,128,1024]{3,2,1,0:T(8,128)(2,1)} %bitcast.70), calls=%async_computation.2 | async-start | bytes 33554432 | tf_op jit(solution)/shard_map/all_to_all | solution.py:47
  159.6 459.2 %all-reduce.2.cloned.1.call-start = ((), (), s32[]{:S(2)}) async-start(), calls=%async_computation.4 | async-start | bytes 4063232 | tf_op jit(solution)/shard_map/psum | solution.py:59
  548.7 10.7 copy-start.4
  548.7 72.5 %copy-start.2 = (f32[31,128]{1,0:T(8,128)S(1)}, f32[31,128]{1,0:T(8,128)}, u32[]{:S(2)}) copy-start(f32[31,128]{1,0:T(8,128)} %param.12) | copy-start | bytes 47620
  705.1 368.6 %all-to-all-start.3 = ((bf16[16,4,128,1024]{3,2,1,0:T(8,128)(2,1)}), bf16[16,4,128,1024]{3,2,1,0:T(8,128)(2,1)}, u32[]{:S(2)}, u32[]{:S(2)}) async-start(bf16[16,4,128,1024]{3,2,1,0:T(8,128)(2,1)} %bitcast.66), calls=%async_computation.3 | async-start | bytes 33554432 | tf_op jit(solution)/shard_map/all_to_all | solution.py:77
  1095.0 78.3 %copy-start.1 = (f32[256]{0:T(256)S(1)}, f32[256]{0:T(256)}, u32[]{:S(2)}) copy-start(f32[256]{0:T(256)} %param.9) | copy-start | bytes 3076
Sparse Core Ops, SparseCore 0:
  558.1 60.7 all-reduce.1
where the time goes:
time: 1190 us; the launch traced here: 1180 us
  waiting for transfers between devices  859 us (72%)
  local copies, waits for them, and re-layouts  131 us (11%)
  matrix products  124 us (10%)
  other arithmetic  27.5 us (2%)
  starting transfers between devices  24.4 us (2%)
  between operations  14.6 us (1%)
    all_to_all x1, waiting for transfers between devices, local(): lax.all_to_all(gamma_send.reshape(groups, capacity, width_pno, width_aux)...  362 us
    all_to_all x1, waiting for transfers between devices, local(): lax.all_to_all(proj_here.reshape(groups, capacity, width_pno, width_aux),...  361 us
    all_to_all x1, waiting for transfers between devices, local(): lax.all_to_all(coef_send.reshape(groups, capacity, width_dom, width_pno),...  76.5 us
    dot_general x1, matrix products, local(): jnp.dot(occ_hot.astype(jnp.bfloat16), terms.reshape(slots, width_dom * wi...  60.6 us
    psum x1, waiting for transfers between devices, local(): coupling = lax.psum(partial_sum, 'aux')  59.4 us
    scatter x1, local copies, waits for them, and re-layouts, local(): jnp.zeros((slots, width_pno, width_aux), jnp.bfloat16).at[slot_of]  41.4 us
  transfers between devices with their start and end apart: 5, of which 4 were waited for; matrix products, arithmetic and copies ran while one was open for 3% of the time, Pallas kernels for 0%

commit v1 on v0

--- a/solution.py
+++ b/solution.py
@@ -56,7 +56,7 @@
     rows_i = paired[:, 0]
     rows_j = paired[:, 1]
     partial_sum = jnp.einsum("kpq,krq->kpr", rows_i, rows_j, preferred_element_type=jnp.float32)
-    coupling = lax.psum(partial_sum, "aux")
+    coupling = jnp.sum(lax.all_gather(partial_sum, "aux"), axis=0)
     fock_i = jnp.take(fock_diag, pair_occ[:, 0])
     fock_j = jnp.take(fock_diag, pair_occ[:, 1])
     denom = pno_energy[:, :, None] + pno_energy[:, None, :] - (fock_i + fock_j)[:, None, None]

time: 1190 us -> 1180 us (level)
    psum x1 -> x0, waiting for transfers between devices: 59.4 us -> none  [local(): coupling = lax.psum(partial_sum, 'aux')]
    all_gather x0 -> x1, waiting for transfers between devices: none -> 53.1 us  [local(): coupling = jnp.sum(lax.all_gather(partial_sum, 'aux'), axis=0)]
where the time goes in v1:
time: 1180 us
  waiting for transfers between devices  853 us (72%)
  local copies, waits for them, and re-layouts  131 us (11%)
  matrix products  124 us (11%)
  other arithmetic  30.8 us (3%)
  starting transfers between devices  24.4 us (2%)
  between operations  14.6 us (1%)
    all_to_all x1, waiting for transfers between devices, local(): lax.all_to_all(gamma_send.reshape(groups, capacity, width_pno, width_aux)...  362 us
    all_to_all x1, waiting for transfers between devices, local(): lax.all_to_all(proj_here.reshape(groups, capacity, width_pno, width_aux),...  361 us
    all_to_all x1, waiting for transfers between devices, local(): lax.all_to_all(coef_send.reshape(groups, capacity, width_dom, width_pno),...  76.4 us
    dot_general x1, matrix products, local(): jnp.dot(occ_hot.astype(jnp.bfloat16), terms.reshape(slots, width_dom * wi...  60.6 us
    all_gather x1, waiting for transfers between devices, local(): coupling = jnp.sum(lax.all_gather(partial_sum, 'aux'), axis=0)  53.1 us
    scatter x1, local copies, waits for them, and re-layouts, local(): jnp.zeros((slots, width_pno, width_aux), jnp.bfloat16).at[slot_of]  41.4 us
  transfers between devices with their start and end apart: 5, of which 4 were waited for; matrix products, arithmetic and copies ran while one was open for 3% of the time, Pallas kernels for 0%

profile of v1, /device:TPU:13, one launch (start us, length us, event | category | flops | bytes accessed | tf_op | source)
XLA Modules:
  0.0 1177.3 jit_solution(12864915644285805620)
XLA Ops:
  10.0 6.5 all-to-all-start.1
  19.6 11.7 scatter_fusion
  31.3 6.4 copy.58
  37.7 6.0 all-to-all-start
  44.0 15.7 %gather_fusion = bf16[64,256,1024]{2,1,0:T(8,128)(2,1)} fusion(bf16[16,256,1024]{2,1,0:T(8,128)(2,1)} %param.8, s32[1024]{0:T(1024)S(1)} %pad_clamp_fusion.3), kind=kCustom, calls=%fused_computation.2 | custom fusion | bytes 67109120 | tf_op jit(solution)/shard_map/jit(_take)/gather | solution.py:32
  59.7 76.4 %all-to-all-done = bf16[16,4,256,128]{2,3,1,0:T(8,128)(2,1)} async-done(((bf16[16,4,256,128]{2,3,1,0:T(8,128)(2,1)}), bf16[16,4,256,128]{2,3,1,0:T(8,128)(2,1)}, u32[]{:S(2)}, u32[]{:S(2)}) %all-to-all-start) | async-done | bytes 4194336 | tf_op jit(solution)/shard_map/all_to_all | solution.py:36
  136.2 18.3 %fusion.10 = bf16[64,128,1024]{2,1,0:T(8,128)(2,1)} fusion(bf16[64,256,128]{1,2,0:T(8,128)(2,1)} %bitcast.4, bf16[64,256,1024]{2,1,0:T(8,128)(2,1)} %gather_fusion, pred[64]{0:T(512)(128)(4,1)S(1)} %broadcast_compare_fusion, pred[64]{0:T(512)(128)(4,1)S(1)} %gt.15), kind=kOutput, calls=%fused_computation.20 | convolution fusion | flops 4336910336 | bytes 54526080 | tf_op jit(solution)/shard_map/sdp,sdq->spq/dot_general | solution.py:44
  154.5 5.2 all-to-all-start.2
  160.1 361.4 %all-to-all-done.2 = bf16[16,4,128,1024]{3,2,1,0:T(8,128)(2,1)} async-done(((bf16[16,4,128,1024]{3,2,1,0:T(8,128)(2,1)}), bf16[16,4,128,1024]{3,2,1,0:T(8,128)(2,1)}, u32[]{:S(2)}, u32[]{:S(2)}) %all-to-all-start.2) | async-done | bytes 16777248 | tf_op jit(solution)/shard_map/all_to_all | solution.py:47
  521.5 13.3 %gather_fusion.1 = bf16[62,128,1024]{2,1,0:T(8,128)(2,1)} fusion(bf16[64,128,1024]{2,1,0:T(8,128)(2,1)} %bitcast.7, s32[1024]{0:T(1024)S(1)} %pad_clamp_fusion.2), kind=kCustom, calls=%fused_computation.3 | custom fusion | bytes 32506104 | tf_op jit(solution)/shard_map/jit(_take)/gather | solution.py:54
  534.8 13.8 %copy_select_fusion = bf16[31,2,128,1024]{3,2,0,1:T(8,128)(2,1)} fusion(bf16[31,2,128,1024]{3,2,1,0:T(8,128)(2,1)} %bitcast.68, pred[31,2]{0,1:T(4,128)(4,1)S(1)} %compare_and_fusion), kind=kLoop, calls=%fused_computation.19 | loop fusion | flops 8126464 | bytes 32505918 | tf_op jit(solution)/shard_map/jit(_take)/select_n | solution.py:54
  548.7 9.2 fusion.14
  559.5 53.1 %all-gather.3.cloned.1.call-done = f32[62,128,128]{2,1,0:T(8,128)} async-done(((f32[31,128,128]{2,1,0:T(8,128)}), f32[62,128,128]{2,1,0:T(8,128)}) %all-gather.3.cloned.1.call-update) | async-done | bytes 4063248 | tf_op jit(solution)/shard_map/all_gather | solution.py:59
  627.2 5.6 convert_bitcast_fusion.1
  632.8 8.9 convert_bitcast_fusion
  641.7 6.2 pad_maximum_fusion
  647.9 6.4 copy.64
  654.3 6.1 broadcast_in_dim.68
  660.4 41.4 %scatter_fusion.1 = bf16[64,128,1024]{2,1,0:T(8,128)(2,1)} fusion(bf16[64,128,1024]{2,1,0:T(8,128)(2,1)} %broadcast_in_dim.68, s32[62]{0:T(128)S(1)} %fusion.28, bf16[62,128,1024]{2,1,0:T(8,128)(2,1)} %bitcast.67), kind=kCustom, calls=%fused_computation.6 | custom fusion | bytes 48759032 | tf_op jit(solution)/shard_map/scatter | solution.py:76
  701.7 6.5 all-to-all-start.3
  708.8 361.6 %all-to-all-done.3 = bf16[16,4,128,1024]{3,2,1,0:T(8,128)(2,1)} async-done(((bf16[16,4,128,1024]{3,2,1,0:T(8,128)(2,1)}), bf16[16,4,128,1024]{3,2,1,0:T(8,128)(2,1)}, u32[]{:S(2)}, u32[]{:S(2)}) %all-to-all-start.3) | async-done | bytes 16777248 | tf_op jit(solution)/shard_map/all_to_all | solution.py:77
  1070.4 21.3 %convolution_convert_fusion = bf16[64,256,1024]{2,1,0:T(8,128)(2,1)} fusion(bf16[64,256,128]{1,2,0:T(8,128)(2,1)} %bitcast.4, bf16[64,128,1024]{2,1,0:T(8,128)(2,1)} %bitcast.20), kind=kOutput, calls=%fused_computation.15 | convolution fusion | flops 4311744512 | bytes 54525952 | tf_op jit(solution)/shard_map/sdp,spq->sdq/dot_general | solution.py:85
  1091.7 60.6 %fusion = f32[16,256,1024]{2,0,1:T(8,128)} fusion(s32[64]{0:T(128)S(1)} %copy-done.5, pred[64]{0:T(512)(128)(4,1)S(1)} %gt.15, bf16[8,8,256,1024]{3,2,1,0:T(8,128)(2,1)} %bitcast.65), kind=kOutput, calls=%fused_computation.7 | convolution fusion | flops 536872960 | bytes 50331968 | tf_op jit(solution)/shard_map/dot_general | solution.py:91
  1152.3 17.8 %copy.67 = f32[16,256,1024]{2,1,0:T(8,128)} copy(f32[16,256,1024]{2,0,1:T(8,128)} %fusion) | data formatting | bytes 33554432
  (50 shorter events, 23.2 us)
Async XLA Ops:
  7.2 550.8 %copy-start = (f32[256]{0:T(256)S(1)}, f32[256]{0:T(256)}, u32[]{:S(2)}) copy-start(f32[256]{0:T(256)} %param.9) | copy-start | bytes 3076
  10.0 27.7 %all-to-all-start.1 = ((s32[16,1,4]{2,1,0:T(1,128)}), s32[16,1,4]{2,1,0:T(1,128)S(1)}, u32[]{:S(2)}, u32[]{:S(2)}) async-start(s32[16,1,4]{2,1,0:T(1,128)} %bitcast.5), calls=%async_computation.1 | async-start | bytes 16384 | tf_op jit(solution)/shard_map/all_to_all | solution.py:27
  37.7 98.5 %all-to-all-start = ((bf16[16,4,256,128]{2,3,1,0:T(8,128)(2,1)}), bf16[16,4,256,128]{2,3,1,0:T(8,128)(2,1)}, u32[]{:S(2)}, u32[]{:S(2)}) async-start(bf16[16,4,256,128]{2,3,1,0:T(8,128)(2,1)} %copy.58), calls=%async_computation | async-start | bytes 8388608 | tf_op jit(solution)/shard_map/all_to_all | solution.py:36
  43.8 15.9 %copy-start.4 = (s32[64]{0:T(128)}, s32[64]{0:T(128)S(1)}, u32[]{:S(2)}) copy-start(s32[64]{0:T(128)S(1)} %max.23) | copy-start | bytes 772
  154.5 5.6 copy-start.3
  154.5 367.0 %all-to-all-start.2 = ((bf16[16,4,128,1024]{3,2,1,0:T(8,128)(2,1)}), bf16[16,4,128,1024]{3,2,1,0:T(8,128)(2,1)}, u32[]{:S(2)}, u32[]{:S(2)}) async-start(bf16[16,4,128,1024]{3,2,1,0:T(8,128)(2,1)} %bitcast.70), calls=%async_computation.2 | async-start | bytes 33554432 | tf_op jit(solution)/shard_map/all_to_all | solution.py:47
  159.7 452.9 %all-gather.3.cloned.1.call-start = ((), (), s32[]{:S(2)}) async-start(), calls=%async_computation.4 | async-start | bytes 6094848 | tf_op jit(solution)/shard_map/all_gather | solution.py:59
  548.7 10.7 copy-start.6
  557.9 65.5 %copy-start.2 = (f32[31,128]{1,0:T(8,128)S(1)}, f32[31,128]{1,0:T(8,128)}, u32[]{:S(2)}) copy-start(f32[31,128]{1,0:T(8,128)} %param.12) | copy-start | bytes 47620
  701.7 368.6 %all-to-all-start.3 = ((bf16[16,4,128,1024]{3,2,1,0:T(8,128)(2,1)}), bf16[16,4,128,1024]{3,2,1,0:T(8,128)(2,1)}, u32[]{:S(2)}, u32[]{:S(2)}) async-start(bf16[16,4,128,1024]{3,2,1,0:T(8,128)(2,1)} %bitcast.66), calls=%async_computation.3 | async-start | bytes 33554432 | tf_op jit(solution)/shard_map/all_to_all | solution.py:77
  1070.4 21.3 %copy-start.5 = (s32[64]{0:T(128)S(1)}, s32[64]{0:T(128)}, u32[]{:S(2)}) copy-start(s32[64]{0:T(128)} %copy-done.4) | copy-start | bytes 772
  1091.7 78.4 %copy-start.1 = (f32[256]{0:T(256)S(1)}, f32[256]{0:T(256)}, u32[]{:S(2)}) copy-start(f32[256]{0:T(256)} %param.9) | copy-start | bytes 3076
Sparse Core Ops, SparseCore 0:
  558.0 54.4 all-gather.2
